TPU v7x, 32 devices: a whole 2x2x4 slice. The times are simulated.
32 devices in a mesh: grp: 2 (over x), sp: 16 (over z, y, core).
Axes of the slice: x: 2, y: 2, z: 4, core: 2. Of those that a mesh axis runs over, the one named last changes fastest.
Arguments:
- latents: bfloat16 [10240, 64], P(('grp', 'sp')), parts along dimension 0, may hold values from -9 to 9
- row_cell: int32 [10240], P(('grp', 'sp')), parts along dimension 0, may hold values from 0 to 5119, as said below
- w_in: bfloat16 [3, 3, 3, 16, 384], replicated, may hold values from -1 to 1
- b_in: float32 [384], replicated, may hold values from -3 to 3
- gain: float32 [384], replicated, may hold values from 0.1 to 1.9
- w_mid: bfloat16 [3, 3, 3, 384, 384], replicated, may hold values from -0.0625 to 0.0625
- b_mid: float32 [384], replicated, may hold values from -3 to 3
Outputs:
- decoded: bfloat16 [32, 2, 4, 160, 384], P(('grp', 'sp')), parts along dimension 0
There are 2 independent parts, one for each index of `grp`. A program takes and returns all parts, laid end to end along the dimension named above; an argument that names none is the same for every part. Nothing has to cross between parts.
Inputs may be any that keep to these rules, and one draw needn't show every extreme that they name: `row_cell`: every token position appears exactly once. The tile of token (t, i, j) is (t // 2) * 8 + (2 i) // 4. Among the tokens of one device, every tile has 20 tokens, except one tile with 40 and one with none; each tile gets 2 * 20 tokens from exactly one device. Order within a device is arbitrary.
All inputs are finite; a program needn't handle non-finite values.
Results may differ from a plain program's by a relative error of at most 0.0051.
Values may be sent and summed in bfloat16 or wider, within the bound.
A program may use at most 128 MiB of HBM per device.

v0:
```python
import jax
import jax.numpy as jnp
from jax import lax
from jax.sharding import PartitionSpec as P

C_LAT = 16
W = 160
TB = 2
HBANDS = 8
HB = 4
TOKS = 320


def passed_along(value, axis, steps):
    count = lax.axis_size(axis)
    pairs = [(source, (source + steps) % count) for source in range(count)]
    return lax.ppermute(value, axis, pairs)


def with_halo(block, sides, width):
    for axis, dim in sides:
        count = lax.axis_size(axis)
        forward = [(i, i + 1) for i in range(count - 1)]
        forward.append((count - 1, 0))
        backward = [(target, source) for source, target in forward]
        low = lax.ppermute(
            lax.slice_in_dim(block, block.shape[dim] - width, None, axis=dim), axis, forward
        )
        high = lax.ppermute(lax.slice_in_dim(block, 0, width, axis=dim), axis, backward)
        block = jnp.concatenate([low, block, high], axis=dim)
    return block


def causal_conv(extended, weight):
    frames_out = extended.shape[0] - 2
    rows_out = extended.shape[1] - 2
    tile_width = extended.shape[2]
    channels = extended.shape[3]
    outputs = weight.shape[4]
    padded = jnp.pad(extended, ((0, 0), (0, 0), (1, 1), (0, 0)))
    widened = jnp.concatenate(
        [padded[:, :, offset : offset + tile_width] for offset in range(3)], axis=3
    )
    accumulated = jnp.zeros((frames_out, rows_out, tile_width, outputs), jnp.float32)
    for tap_time in range(3):
        for tap_row in range(3):
            window = widened[tap_time : tap_time + frames_out, tap_row : tap_row + rows_out]
            kernel = weight[tap_time, tap_row].reshape(3 * channels, outputs)
            accumulated = accumulated + jnp.einsum(
                "thwc,cd->thwd", window, kernel, preferred_element_type=jnp.float32
            )
    return accumulated


def rms_silu(hidden, gain):
    values = hidden.astype(jnp.float32)
    inverse_rms = lax.rsqrt(jnp.mean(values * values, axis=-1, keepdims=True) + 1e-06)
    return jax.nn.silu(values * inverse_rms * gain).astype(jnp.bfloat16)


def band_mask(extended, band_index, margin):
    row_count = extended.shape[1]
    global_row = band_index * HB - margin + jnp.arange(row_count, dtype=jnp.int32)
    inside = (global_row >= 0) & (global_row < HB * HBANDS)
    return jnp.where(inside[None, :, None, None], extended, jnp.zeros((), extended.dtype))


def keep_when(flag, values):
    return jnp.where(flag, values, jnp.zeros((), values.dtype))


def margin_tail(rimmed, band_index, time_block, w_in, b_in, gain):
    hidden_wide = (causal_conv(rimmed, w_in) + b_in).astype(jnp.bfloat16)
    active_wide = band_mask(rms_silu(hidden_wide, gain), band_index, 1)
    frame_valid = time_block * TB - 2 + jnp.arange(TB + 2, dtype=jnp.int32) >= 0
    activated = jnp.where(
        frame_valid[:, None, None, None], active_wide, jnp.zeros((), active_wide.dtype)
    )
    return (activated, hidden_wide[2:, 1:-1])


def shards(latents, row_cell, w_in, b_in, gain, w_mid, b_mid):
    devices = lax.axis_size("sp")
    position = lax.axis_index("sp")
    offset_tiles = 2 * HBANDS + HBANDS // 2
    tile_index = (position + offset_tiles) % devices
    band_index = tile_index % HBANDS
    time_block = tile_index // HBANDS
    slot_count = 2 * (TOKS // devices)
    half_rows = HB // 2
    half_width = W // 2
    channels_in = latents.shape[1]
    column = row_cell % half_width
    token_row = row_cell // half_width % (half_rows * HBANDS)
    frame_index = row_cell // (half_width * half_rows * HBANDS)
    owner_tile = frame_index // TB * HBANDS + token_row // half_rows
    frame_within = frame_index % TB
    row_within = token_row % half_rows
    local_index = (frame_within * half_rows + row_within) * half_width + column
    owner_hits = (owner_tile[:, None] == jnp.arange(devices, dtype=jnp.int32)[None, :]).astype(
        jnp.int32
    )
    earlier = jnp.cumsum(owner_hits, axis=0) - owner_hits
    slot_rank = jnp.sum(earlier * owner_hits, axis=1)
    owner_device = (owner_tile - offset_tiles) % devices
    target = owner_device * slot_count + slot_rank
    outgoing = jnp.zeros((devices * slot_count, channels_in), latents.dtype).at[target].set(latents)
    places = jnp.full((devices * slot_count,), TOKS, jnp.int32).at[target].set(local_index)
    arrived, arrived_places = (
        lax.all_to_all(
            outgoing.reshape(devices, slot_count, channels_in),
            "sp",
            split_axis=0,
            concat_axis=0,
            tiled=True,
        ),
        lax.all_to_all(
            places.reshape(devices, slot_count), "sp", split_axis=0, concat_axis=0, tiled=True
        ),
    )
    flat_arrived = arrived.reshape(devices * slot_count, channels_in)
    flat_places = arrived_places.reshape(-1)
    tile_tokens = (
        jnp.zeros((TOKS, channels_in), latents.dtype).at[flat_places].set(flat_arrived, mode="drop")
    )
    latent_grid = tile_tokens.reshape(TB, half_rows, half_width, 2, 2, C_LAT)
    latent_grid = latent_grid.transpose(0, 1, 3, 2, 4, 5).reshape(TB, HB, W, C_LAT)
    prior_block = keep_when(time_block >= 1, passed_along(latent_grid, "sp", HBANDS))
    older_block = keep_when(time_block >= 2, passed_along(latent_grid, "sp", 2 * HBANDS))
    stacked = jnp.concatenate([older_block, prior_block, latent_grid], axis=0)
    rimmed = band_mask(with_halo(stacked, (("sp", 1),), 2), band_index, 2)
    activated, hidden = margin_tail(rimmed, band_index, time_block, w_in, b_in, gain)
    mixed = causal_conv(activated, w_mid) + b_mid + hidden.astype(jnp.float32)
    return mixed.astype(jnp.bfloat16)[None]


def solution(mesh):
    return jax.shard_map(
        shards,
        mesh=mesh,
        in_specs=(P(("grp", "sp"), None), P(("grp", "sp")), P(), P(), P(), P(), P()),
        out_specs=P(("grp", "sp"), None, None, None, None),
        check_vma=False,
    )
```

profile of v0, /device:TPU:0, one launch (start us, length us, event | category | flops | bytes accessed | tf_op | source)
XLA Modules:
  0.0 124.3 jit_solution(10751556660676795817)
XLA Ops:
  0.0 0.7 fusion.27
  0.7 0.9 reduce-window.6
  1.6 0.2 slice_reduce_fusion
  2.0 2.9 %scatter_custom_fusion = s32[640]{0:T(1024)S(1)} fusion(s32[320]{0:T(512)S(1)} %compare_select_fusion.1, s32[320]{0:T(512)S(1)} %get-tuple-element.29, s32[]{:T(128)} %constant.143.clone.1), kind=kCustom, calls=%fused_computation.79 | custom fusion | bytes 2564 | tf_op jit(solution)/shard_map/scatter | solution.py:108
  4.9 0.7 all_to_all.9
  5.6 7.4 %all-to-all-start = ((s32[16,1,40]{2,1,0:T(1,128)}), s32[16,1,40]{2,1,0:T(1,128)S(1)}, u32[]{:S(2)}, u32[]{:S(2)}) async-start(s32[16,1,40]{2,1,0:T(1,128)} %all_to_all.9), calls=%async_computation | async-start | bytes 16384 | tf_op jit(solution)/shard_map/all_to_all | solution.py:117
  13.1 5.4 %fusion.41 = (bf16[1,1,3,384,384]{4,3,2,1,0:T(8,128)(2,1)}, bf16[1,1,3,384,384]{4,3,2,1,0:T(8,128)(2,1)}, bf16[1,1,3,384,384]{4,3,2,1,0:T(8,128)(2,1)}, bf16[1,1...) fusion(bf16[3,3,3,384,384]{4,3,2,1,0:T(8,128)(2,1)} %param.12), kind=kLoop, calls=%fused_computation.98 | loop fusion | bytes 15925248 | tf_op jit(solution)/shard_map/slice | solution.py:48
  18.6 0.1 copy.18
  18.7 1.4 %scatter_custom_fusion.1 = bf16[640,64]{1,0:T(8,128)(2,1)S(1)} fusion(s32[320]{0:T(512)S(1)} %compare_select_fusion.1, bf16[320,64]{1,0:T(8,128)(2,1)S(1)} %copy.18, bf16[]{:T(256)} %constant.142.clone.1), kind=kCustom, calls=%fused_computation.26 | custom fusion | bytes 81922 | tf_op jit(solution)/shard_map/scatter | solution.py:107
  20.1 0.8 reshape.159
  20.8 6.0 %all-to-all-start.1 = ((bf16[16,2,1280]{2,1,0:T(2,128)(2,1)}), bf16[16,2,1280]{2,1,0:T(2,128)(2,1)S(1)}, u32[]{:S(2)}, u32[]{:S(2)}) async-start(bf16[16,2,1280]{2,1,0:T(2,128)(2,1)} %reshape.159), calls=%async_computation.1 | async-start | bytes 163840 | tf_op jit(solution)/shard_map/all_to_all | solution.py:110
  26.9 0.5 broadcast.176
  27.4 0.6 reduce.7
  28.0 0.1 reshape.92
  28.1 5.9 %all-to-all-done.1 = bf16[16,2,1280]{2,1,0:T(2,128)(2,1)S(1)} async-done(((bf16[16,2,1280]{2,1,0:T(2,128)(2,1)}), bf16[16,2,1280]{2,1,0:T(2,128)(2,1)S(1)}, u32[]{:S(2)}, u32[]{:S(2)}) %all-to-all-start.1) | async-done | bytes 81952 | tf_op jit(solution)/shard_map/all_to_all | solution.py:110
  34.0 0.2 reshape.160
  34.1 4.2 %scatter_custom_fusion.2 = bf16[320,64]{1,0:T(8,128)(2,1)S(1)} fusion(s32[640]{0:T(1024)S(1)} %fusion.17, bf16[640,64]{1,0:T(8,128)(2,1)S(1)} %bitcast.153, bf16[]{:T(256)} %constant.142.clone.1), kind=kCustom, calls=%fused_computation.30 | custom fusion | bytes 40962 | tf_op jit(solution)/shard_map/scatter | solution.py:124
  38.4 0.1 copy.19
  38.5 0.1 reshape.95
  38.6 0.2 copy.20
  38.8 0.2 copy.21
  39.0 0.2 collective-permute-start.1
  39.2 5.6 %collective-permute-done.1 = bf16[2,4,160,16]{2,3,1,0:T(8,128)(2,1)S(1)} collective-permute-done((bf16[2,4,160,16]{2,3,1,0:T(8,128)(2,1)S(1)}, bf16[2,4,160,16]{2,3,1,0:T(8,128)(2,1)S(1)}, u32[]{:S(2)}, u32[]{:S(2)}) %collective-permute-start.1) | collective-permute-done | bytes 40992 | tf_op jit(solution)/shard_map/ppermute | solution.py:17
  45.0 4.4 %collective-permute-start.3 = (bf16[6,2,160,16]{2,3,1,0:T(8,128)(2,1)S(1)}, bf16[6,2,160,16]{2,3,1,0:T(8,128)(2,1)S(1)}, u32[]{:S(2)}, u32[]{:S(2)}) collective-permute-start(bf16[6,2,160,16]{2,3,1,0:T(8,128)(2,1)S(1)} %get-tuple-element.28), channel_id=1, source_target_pairs={{1,0},{2,1},{3,2},{4,3},{5,4},{6,5},{7,6},{8,7},{9,8},{10,9},{11,1... | collective-permute-start | bytes 184328 | tf_op jit(solution)/shard_map/ppermute | solution.py:29
  49.4 2.3 %collective-permute-done.2 = bf16[6,2,160,16]{2,3,1,0:T(8,128)(2,1)S(1)} collective-permute-done((bf16[6,2,160,16]{2,3,1,0:T(8,128)(2,1)S(1)}, bf16[6,2,160,16]{2,3,1,0:T(8,128)(2,1)S(1)}, u32[]{:S(2)}, u32[]{:S(2)}) %collective-permute-start.2) | collective-permute-done | bytes 61472 | tf_op jit(solution)/shard_map/ppermute | solution.py:26
  51.7 0.1 maximum_select_fusion
  51.8 0.3 pad_slice_fusion.3
  52.2 3.5 %fusion.39 = f32[4,6,160,384]{3,2,1,0:T(8,128)} fusion(bf16[48,384,1,1]{1,0,3,2:T(8,128)(2,1)S(1)} %bitcast.162, bf16[6,8,160,16]{2,3,1,0:T(8,128)(2,1)S(1)} %get-tuple-element.17, bf16[6,8,160,16]{2,3,1,0:T(8,128)(2,1)S(1)} %maximum_select_fusion, bf16[6,8,160,16]{2,3,1,0:T(8,128)(2,1)S(1)} %get-tuple-element.16), kind=kOutput, calls=%fused_computation.96 | convolution fusion | flops 143769600 | bytes 6672384 | tf_op jit(solution)/shard_map/thwc,cd->thwd/dot_general | solution.py:49
  55.7 3.5 %fusion.38 = f32[4,6,160,384]{3,2,1,0:T(8,128)} fusion(bf16[48,384,1,1]{1,0,3,2:T(8,128)(2,1)S(1)} %bitcast.161, bf16[6,8,160,16]{2,3,1,0:T(8,128)(2,1)S(1)} %get-tuple-element.17, bf16[6,8,160,16]{2,3,1,0:T(8,128)(2,1)S(1)} %maximum_select_fusion, bf16[6,8,160,16]{2,3,1,0:T(8,128)(2,1)S(1)} %get-tuple-element.16), kind=kOutput, calls=%fused_computation.95 | convolution fusion | flops 143769600 | bytes 6672384 | tf_op jit(solution)/shard_map/thwc,cd->thwd/dot_general | solution.py:49
  59.1 3.4 %fusion.37 = f32[4,6,160,384]{3,2,1,0:T(8,128)} fusion(bf16[48,384,1,1]{1,0,3,2:T(8,128)(2,1)S(1)} %bitcast.160, bf16[6,8,160,16]{2,3,1,0:T(8,128)(2,1)S(1)} %get-tuple-element.17, bf16[6,8,160,16]{2,3,1,0:T(8,128)(2,1)S(1)} %maximum_select_fusion, bf16[6,8,160,16]{2,3,1,0:T(8,128)(2,1)S(1)} %get-tuple-element.16), kind=kOutput, calls=%fused_computation.94 | convolution fusion | flops 143769600 | bytes 6672384 | tf_op jit(solution)/shard_map/thwc,cd->thwd/dot_general | solution.py:49
  62.6 3.5 %fusion.36 = f32[4,6,160,384]{3,2,1,0:T(8,128)} fusion(bf16[48,384,1,1]{1,0,3,2:T(8,128)(2,1)S(1)} %bitcast.159, bf16[6,8,160,16]{2,3,1,0:T(8,128)(2,1)S(1)} %get-tuple-element.17, bf16[6,8,160,16]{2,3,1,0:T(8,128)(2,1)S(1)} %maximum_select_fusion, bf16[6,8,160,16]{2,3,1,0:T(8,128)(2,1)S(1)} %get-tuple-element.16), kind=kOutput, calls=%fused_computation.93 | convolution fusion | flops 143769600 | bytes 6672384 | tf_op jit(solution)/shard_map/thwc,cd->thwd/dot_general | solution.py:49
  66.1 3.5 %fusion.35 = f32[4,6,160,384]{3,2,1,0:T(8,128)} fusion(bf16[48,384,1,1]{1,0,3,2:T(8,128)(2,1)S(1)} %bitcast.158, bf16[6,8,160,16]{2,3,1,0:T(8,128)(2,1)S(1)} %get-tuple-element.17, bf16[6,8,160,16]{2,3,1,0:T(8,128)(2,1)S(1)} %maximum_select_fusion, bf16[6,8,160,16]{2,3,1,0:T(8,128)(2,1)S(1)} %get-tuple-element.16), kind=kOutput, calls=%fused_computation.92 | convolution fusion | flops 143769600 | bytes 6672384 | tf_op jit(solution)/shard_map/thwc,cd->thwd/dot_general | solution.py:49
  69.6 3.6 %fusion.34 = f32[4,6,160,384]{3,2,1,0:T(8,128)} fusion(bf16[48,384,1,1]{1,0,3,2:T(8,128)(2,1)S(1)} %bitcast.157, bf16[6,8,160,16]{2,3,1,0:T(8,128)(2,1)S(1)} %get-tuple-element.17, bf16[6,8,160,16]{2,3,1,0:T(8,128)(2,1)S(1)} %maximum_select_fusion, bf16[6,8,160,16]{2,3,1,0:T(8,128)(2,1)S(1)} %get-tuple-element.16), kind=kOutput, calls=%fused_computation.91 | convolution fusion | flops 143769600 | bytes 6672384 | tf_op jit(solution)/shard_map/thwc,cd->thwd/dot_general | solution.py:49
  73.1 3.5 %fusion.33 = f32[4,6,160,384]{3,2,1,0:T(8,128)} fusion(bf16[48,384,1,1]{1,0,3,2:T(8,128)(2,1)S(1)} %bitcast.156, bf16[6,8,160,16]{2,3,1,0:T(8,128)(2,1)S(1)} %get-tuple-element.17, bf16[6,8,160,16]{2,3,1,0:T(8,128)(2,1)S(1)} %maximum_select_fusion, bf16[6,8,160,16]{2,3,1,0:T(8,128)(2,1)S(1)} %get-tuple-element.16), kind=kOutput, calls=%fused_computation.90 | convolution fusion | flops 143769600 | bytes 6672384 | tf_op jit(solution)/shard_map/thwc,cd->thwd/dot_general | solution.py:49
  76.6 3.5 %fusion.40 = f32[4,6,160,384]{3,2,1,0:T(8,128)} fusion(bf16[48,384,1,1]{1,0,3,2:T(8,128)(2,1)S(1)} %bitcast.155, bf16[6,8,160,16]{2,3,1,0:T(8,128)(2,1)S(1)} %get-tuple-element.17, bf16[6,8,160,16]{2,3,1,0:T(8,128)(2,1)S(1)} %maximum_select_fusion, bf16[6,8,160,16]{2,3,1,0:T(8,128)(2,1)S(1)} %get-tuple-element.16), kind=kOutput, calls=%fused_computation.97 | convolution fusion | flops 143769600 | bytes 6672384 | tf_op jit(solution)/shard_map/thwc,cd->thwd/dot_general | solution.py:49
  80.1 17.7 %fusion = (f32[4,6,160]{2,1,0:T(8,128)S(1)}, bf16[4,6,160,384]{3,2,1,0:T(8,128)(2,1)}) fusion(f32[384]{0:T(512)S(1)} %copy-done.11, bf16[48,384,1,1]{1,0,3,2:T(8,128)(2,1)S(1)} %bitcast.154, bf16[6,8,160,16]{2,3,1,0:T(8,128)(2,1)S(1)} %get-tuple-element.17, bf16[6,8,160,16]{2,3,1,0:T(8,128)(2,1)S(1)} %maximum_select_fusion, ...), kind=kOutput, calls=%fused_computation.6 | convolution fusion | flops 162935040 | bytes 50926080 | tf_op jit(solution)/shard_map/thwc,cd->thwd/dot_general | solution.py:49
  97.8 3.6 %fusion.9 = bf16[4,6,160,384]{3,2,1,0:T(8,128)(2,1)S(1)} fusion(bf16[4,6,160,384]{3,2,1,0:T(8,128)(2,1)} %get-tuple-element.32, f32[384]{0:T(512)S(1)} %copy-done.10, f32[4,6,160]{2,1,0:T(8,128)S(1)} %add_rsqrt_fusion, pred[6]{0:T(512)(128)(4,1)S(1)} %compare_and_fusion.1, pred[4]{0:T(512)(128)(4,1)S(1)} %add_compare_fusion), kind=kLoop, calls=%fused_computation.16 | loop fusion | flops 14745600 | bytes 5915146 | tf_op jit(solution)/shard_map/jit(_where)/select_n | solution.py:76
  101.4 2.5 %pad_slice_fusion.1 = (bf16[4,6,160,384]{3,2,1,0:T(8,128)(2,1)S(1)}, bf16[4,6,160,384]{3,2,1,0:T(8,128)(2,1)S(1)}) fusion(bf16[4,6,160,384]{3,2,1,0:T(8,128)(2,1)S(1)} %fusion.9), kind=kLoop, calls=%fused_computation.18 | loop fusion | bytes 8847360 | tf_op jit(solution)/shard_map/slice | solution.py:42
  103.9 1.1 pad_maximum_fusion
  105.1 1.8 %fusion.50 = f32[2,4,160,384]{3,2,1,0:T(8,128)S(1)} fusion(bf16[4,6,160,1152]{3,2,1,0:T(8,128)(2,1)S(1)} %pad_maximum_fusion, bf16[1152,384,1,1]{1,0,3,2:T(8,128)(2,1)S(1)} %bitcast.150), kind=kOutput, calls=%fused_computation.107 | convolution fusion | flops 1132462080 | bytes 11698176 | tf_op jit(solution)/shard_map/thwc,cd->thwd/dot_general | solution.py:49
  106.9 1.8 %fusion.45 = f32[2,4,160,384]{3,2,1,0:T(8,128)S(1)} fusion(bf16[4,6,160,1152]{3,2,1,0:T(8,128)(2,1)S(1)} %pad_maximum_fusion, bf16[1152,384,1,1]{1,0,3,2:T(8,128)(2,1)S(1)} %bitcast.149), kind=kOutput, calls=%fused_computation.102 | convolution fusion | flops 1132462080 | bytes 11698176 | tf_op jit(solution)/shard_map/thwc,cd->thwd/dot_general | solution.py:49
  108.7 1.8 %fusion.49 = f32[2,4,160,384]{3,2,1,0:T(8,128)S(1)} fusion(bf16[4,6,160,1152]{3,2,1,0:T(8,128)(2,1)S(1)} %pad_maximum_fusion, bf16[1152,384,1,1]{1,0,3,2:T(8,128)(2,1)S(1)} %bitcast.148), kind=kOutput, calls=%fused_computation.106 | convolution fusion | flops 1132462080 | bytes 11698176 | tf_op jit(solution)/shard_map/thwc,cd->thwd/dot_general | solution.py:49
  110.5 1.8 %fusion.48 = f32[2,4,160,384]{3,2,1,0:T(8,128)S(1)} fusion(bf16[4,6,160,1152]{3,2,1,0:T(8,128)(2,1)S(1)} %pad_maximum_fusion, bf16[1152,384,1,1]{1,0,3,2:T(8,128)(2,1)S(1)} %bitcast.147), kind=kOutput, calls=%fused_computation.105 | convolution fusion | flops 1132462080 | bytes 11698176 | tf_op jit(solution)/shard_map/thwc,cd->thwd/dot_general | solution.py:49
  112.3 1.8 %fusion.47 = f32[2,4,160,384]{3,2,1,0:T(8,128)S(1)} fusion(bf16[4,6,160,1152]{3,2,1,0:T(8,128)(2,1)S(1)} %pad_maximum_fusion, bf16[1152,384,1,1]{1,0,3,2:T(8,128)(2,1)S(1)} %bitcast.146), kind=kOutput, calls=%fused_computation.104 | convolution fusion | flops 1132462080 | bytes 11698176 | tf_op jit(solution)/shard_map/thwc,cd->thwd/dot_general | solution.py:49
  114.1 1.8 %fusion.46 = f32[2,4,160,384]{3,2,1,0:T(8,128)S(1)} fusion(bf16[4,6,160,1152]{3,2,1,0:T(8,128)(2,1)S(1)} %pad_maximum_fusion, bf16[1152,384,1,1]{1,0,3,2:T(8,128)(2,1)S(1)} %bitcast.145), kind=kOutput, calls=%fused_computation.103 | convolution fusion | flops 1132462080 | bytes 11698176 | tf_op jit(solution)/shard_map/thwc,cd->thwd/dot_general | solution.py:49
  115.9 1.8 %fusion.44 = f32[2,4,160,384]{3,2,1,0:T(8,128)S(1)} fusion(bf16[4,6,160,1152]{3,2,1,0:T(8,128)(2,1)S(1)} %pad_maximum_fusion, bf16[1152,384,1,1]{1,0,3,2:T(8,128)(2,1)S(1)} %bitcast.144), kind=kOutput, calls=%fused_computation.101 | convolution fusion | flops 1132462080 | bytes 11698176 | tf_op jit(solution)/shard_map/thwc,cd->thwd/dot_general | solution.py:49
  117.7 1.8 %fusion.51 = f32[2,4,160,384]{3,2,1,0:T(8,128)S(1)} fusion(bf16[4,6,160,1152]{3,2,1,0:T(8,128)(2,1)S(1)} %pad_maximum_fusion, bf16[1152,384,1,1]{1,0,3,2:T(8,128)(2,1)S(1)} %bitcast.143), kind=kOutput, calls=%fused_computation.108 | convolution fusion | flops 1132462080 | bytes 11698176 | tf_op jit(solution)/shard_map/thwc,cd->thwd/dot_general | solution.py:49
  119.5 4.8 %fusion.10 = bf16[1,2,4,160,384]{4,3,2,1,0:T(8,128)(2,1)} fusion(bf16[4,6,160,1152]{3,2,1,0:T(8,128)(2,1)S(1)} %pad_maximum_fusion, bf16[1152,384,1,1]{1,0,3,2:T(8,128)(2,1)S(1)} %bitcast.141, f32[2,4,160,384]{3,2,1,0:T(8,128)S(1)} %fusion.51, f32[2,4,160,384]{3,2,1,0:T(8,128)S(1)} %fusion.50, f32[2,4,160,384]{3,2,1,0:T(8,128)S(1)} %fusion.49, ...), kind=kOutput, calls=%fused_computation.20 | convolution fusion | flops 1138360320 | bytes 27428352 | tf_op jit(solution)/shard_map/thwc,cd->thwd/dot_general | solution.py:49
  (45 shorter events, 0.5 us)
Async XLA Ops:
  5.6 15.2 %all-to-all-start = ((s32[16,1,40]{2,1,0:T(1,128)}), s32[16,1,40]{2,1,0:T(1,128)S(1)}, u32[]{:S(2)}, u32[]{:S(2)}) async-start(s32[16,1,40]{2,1,0:T(1,128)} %all_to_all.9), calls=%async_computation | async-start | bytes 16384 | tf_op jit(solution)/shard_map/all_to_all | solution.py:117
  13.0 5.4 %copy-start.7 = (bf16[3,3,3,16,384]{4,3,2,1,0:T(8,128)(2,1)S(1)}, bf16[3,3,3,16,384]{4,3,2,1,0:T(8,128)(2,1)}, u32[]{:S(2)}) copy-start(bf16[3,3,3,16,384]{4,3,2,1,0:T(8,128)(2,1)} %param.9) | copy-start | bytes 995332
  13.1 5.5 %copy-start.8 = (bf16[320,64]{0,1:T(8,128)(2,1)S(1)}, bf16[320,64]{0,1:T(8,128)(2,1)}, u32[]{:S(2)}) copy-start(bf16[320,64]{0,1:T(8,128)(2,1)} %param.7) | copy-start | bytes 122884
  20.8 13.1 %all-to-all-start.1 = ((bf16[16,2,1280]{2,1,0:T(2,128)(2,1)}), bf16[16,2,1280]{2,1,0:T(2,128)(2,1)S(1)}, u32[]{:S(2)}, u32[]{:S(2)}) async-start(bf16[16,2,1280]{2,1,0:T(2,128)(2,1)} %reshape.159), calls=%async_computation.1 | async-start | bytes 163840 | tf_op jit(solution)/shard_map/all_to_all | solution.py:110
  39.0 5.8 %collective-permute-start.1 = (bf16[2,4,160,16]{2,3,1,0:T(8,128)(2,1)S(1)}, bf16[2,4,160,16]{2,3,1,0:T(8,128)(2,1)S(1)}, u32[]{:S(2)}, u32[]{:S(2)}) collective-permute-start(bf16[2,4,160,16]{2,3,1,0:T(8,128)(2,1)S(1)} %copy.21), channel_id=1, source_target_pairs={{0,8},{1,9},{2,10},{3,11},{4,12},{5,13},{6,14},{7,15},{8,0},{9,1},... | collective-permute-start | bytes 122888 | tf_op jit(solution)/shard_map/ppermute | solution.py:17
  39.2 5.6 %collective-permute-start = (bf16[2,4,160,16]{2,3,1,0:T(8,128)(2,1)S(1)}, bf16[2,4,160,16]{2,3,1,0:T(8,128)(2,1)S(1)}, u32[]{:S(2)}, u32[]{:S(2)}) collective-permute-start(bf16[2,4,160,16]{2,3,1,0:T(8,128)(2,1)S(1)} %copy.21), channel_id=1, source_target_pairs={{0,0},{1,1},{2,2},{3,3},{4,4},{5,5},{6,6},{7,7},{8,8},{9,9},{10,10... | collective-permute-start | bytes 122888 | tf_op jit(solution)/shard_map/ppermute | solution.py:17
  44.9 6.8 %collective-permute-start.2 = (bf16[6,2,160,16]{2,3,1,0:T(8,128)(2,1)S(1)}, bf16[6,2,160,16]{2,3,1,0:T(8,128)(2,1)S(1)}, u32[]{:S(2)}, u32[]{:S(2)}) collective-permute-start(bf16[6,2,160,16]{2,3,1,0:T(8,128)(2,1)S(1)} %get-tuple-element.27), channel_id=1, source_target_pairs={{0,1},{1,2},{2,3},{3,4},{4,5},{5,6},{6,7},{7,8},{8,9},{9,10},{10,1... | collective-permute-start | bytes 184328 | tf_op jit(solution)/shard_map/ppermute | solution.py:26
  45.0 6.7 %collective-permute-start.3 = (bf16[6,2,160,16]{2,3,1,0:T(8,128)(2,1)S(1)}, bf16[6,2,160,16]{2,3,1,0:T(8,128)(2,1)S(1)}, u32[]{:S(2)}, u32[]{:S(2)}) collective-permute-start(bf16[6,2,160,16]{2,3,1,0:T(8,128)(2,1)S(1)} %get-tuple-element.28), channel_id=1, source_target_pairs={{1,0},{2,1},{3,2},{4,3},{5,4},{6,5},{7,6},{8,7},{9,8},{10,9},{11,1... | collective-permute-start | bytes 184328 | tf_op jit(solution)/shard_map/ppermute | solution.py:29
  76.6 3.5 %copy-start.11 = (f32[384]{0:T(512)S(1)}, f32[384]{0:T(512)}, u32[]{:S(2)}) copy-start(f32[384]{0:T(512)} %param.10) | copy-start | bytes 4612
  80.1 17.7 %copy-start.10 = (f32[384]{0:T(512)S(1)}, f32[384]{0:T(512)}, u32[]{:S(2)}) copy-start(f32[384]{0:T(512)} %param.11) | copy-start | bytes 4612
  103.9 1.2 copy-start.6
  105.1 1.8 %copy-start.5 = (bf16[1,1,3,384,384]{4,3,2,1,0:T(8,128)(2,1)S(1)}, bf16[1,1,3,384,384]{4,3,2,1,0:T(8,128)(2,1)}, u32[]{:S(2)}) copy-start(bf16[1,1,3,384,384]{4,3,2,1,0:T(8,128)(2,1)} %get-tuple-element.5) | copy-start | bytes 2654212
  106.9 1.8 %copy-start.4 = (bf16[1,1,3,384,384]{4,3,2,1,0:T(8,128)(2,1)S(1)}, bf16[1,1,3,384,384]{4,3,2,1,0:T(8,128)(2,1)}, u32[]{:S(2)}) copy-start(bf16[1,1,3,384,384]{4,3,2,1,0:T(8,128)(2,1)} %get-tuple-element.7) | copy-start | bytes 2654212
  108.7 1.8 %copy-start.3 = (bf16[1,1,3,384,384]{4,3,2,1,0:T(8,128)(2,1)S(1)}, bf16[1,1,3,384,384]{4,3,2,1,0:T(8,128)(2,1)}, u32[]{:S(2)}) copy-start(bf16[1,1,3,384,384]{4,3,2,1,0:T(8,128)(2,1)} %get-tuple-element.8) | copy-start | bytes 2654212
  110.5 1.8 %copy-start.2 = (bf16[1,1,3,384,384]{4,3,2,1,0:T(8,128)(2,1)S(1)}, bf16[1,1,3,384,384]{4,3,2,1,0:T(8,128)(2,1)}, u32[]{:S(2)}) copy-start(bf16[1,1,3,384,384]{4,3,2,1,0:T(8,128)(2,1)} %get-tuple-element.9) | copy-start | bytes 2654212
  112.3 1.8 %copy-start.1 = (bf16[1,1,3,384,384]{4,3,2,1,0:T(8,128)(2,1)S(1)}, bf16[1,1,3,384,384]{4,3,2,1,0:T(8,128)(2,1)}, u32[]{:S(2)}) copy-start(bf16[1,1,3,384,384]{4,3,2,1,0:T(8,128)(2,1)} %get-tuple-element.10) | copy-start | bytes 2654212
  114.1 1.8 %copy-start = (bf16[1,1,3,384,384]{4,3,2,1,0:T(8,128)(2,1)S(1)}, bf16[1,1,3,384,384]{4,3,2,1,0:T(8,128)(2,1)}, u32[]{:S(2)}) copy-start(bf16[1,1,3,384,384]{4,3,2,1,0:T(8,128)(2,1)} %get-tuple-element.11) | copy-start | bytes 2654212
  117.7 1.8 %copy-start.9 = (f32[384]{0:T(512)S(1)}, f32[384]{0:T(512)}, u32[]{:S(2)}) copy-start(f32[384]{0:T(512)} %param.13) | copy-start | bytes 4612
where the time goes:
time: 125 us; the launch traced here: 124 us
  matrix products  64.6 us (52%)
  local copies, waits for them, and re-layouts  20 us (16%)
  starting transfers between devices  18.1 us (14%)
  waiting for transfers between devices  13.8 us (11%)
  other arithmetic  7.33 us (6%)
    dot_general x18, matrix products, causal_conv(): jnp.einsum('thwc,cd->thwd', window, kernel, preferred_element_type=jnp.fl...  64.6 us
    all_to_all x1, starting transfers between devices, shards(): lax.all_to_all(places.reshape(devices, slot_count), 'sp', split_axis=0, c...  7.41 us
    all_to_all x1, starting transfers between devices, shards(): lax.all_to_all(outgoing.reshape(devices, slot_count, channels_in), 'sp',...  6.01 us
    all_to_all x1, waiting for transfers between devices, shards(): lax.all_to_all(outgoing.reshape(devices, slot_count, channels_in), 'sp',...  5.88 us
    ppermute x2, waiting for transfers between devices, passed_along(): return lax.ppermute(value, axis, pairs)  5.62 us
    slice x2, local copies, waits for them, and re-layouts, causal_conv(): kernel = weight[tap_time, tap_row].reshape(3 * channels, outputs)  5.44 us
    ppermute x1, starting transfers between devices, with_halo(): lax.ppermute(lax.slice_in_dim(block, 0, width, axis=dim), axis, backward)  4.43 us
    scatter x2, local copies, waits for them, and re-layouts, shards(): jnp.zeros((TOKS, channels_in), latents.dtype).at[flat_places]  4.32 us
  transfers between devices with their start and end apart: 6, of which 3 were waited for; matrix products, arithmetic and copies ran while one was open for 7% of the time, Pallas kernels for 0%

commit v1 on v0

v1 whole, which is shorter than its diff:
```python
import functools

import jax
import jax.numpy as jnp
from jax import lax
from jax.experimental import pallas as pl
from jax.experimental.pallas import tpu as pltpu
from jax.sharding import PartitionSpec as P

C_LAT = 16
W = 160
TB = 2
HBANDS = 8
HB = 4
HALF_ROWS = HB // 2
HALF_W = W // 2
OFFSET_TILES = 2 * HBANDS + HBANDS // 2
F32 = jnp.float32
BF16 = jnp.bfloat16


def iota(shape, dim):
    return lax.broadcasted_iota(jnp.int32, shape, dim)


def dot(a, b, dims=((1,), (0,))):
    return lax.dot_general(a, b, (dims, ((), ())), preferred_element_type=F32)


def gather_kernel(n, slots, depth, lat_ref, cell_ref, out_ref, pack, arrived, mine, near,
                  send_a, recv_a, send_b, recv_b):
    me = lax.axis_index("sp")
    toks = lat_ref.shape[0]
    barrier = pltpu.get_barrier_semaphore()
    for delta in range(1, n):
        pl.semaphore_signal(
            barrier, inc=1, device_id={"sp": lax.rem(me + delta, n)},
            device_id_type=pl.DeviceIdType.MESH,
        )
    cell = cell_ref[...].astype(F32)
    line = jnp.floor((cell + 0.5) * (1.0 / HALF_W))
    column = cell - HALF_W * line
    token_rows = HALF_ROWS * HBANDS
    frame = jnp.floor((line + 0.5) * (1.0 / token_rows))
    token_row = line - token_rows * frame
    time_block = jnp.floor((frame + 0.5) * (1.0 / TB))
    band = jnp.floor((token_row + 0.5) * (1.0 / HALF_ROWS))
    place_row = (frame - TB * time_block) * HALF_ROWS + token_row - HALF_ROWS * band
    owner = time_block * HBANDS + band - (OFFSET_TILES % n)
    owner = jnp.where(owner < 0, owner + n, owner)
    hits = owner == iota((n, toks), 0).astype(F32)
    hits = jnp.where(hits, 1.0, 0.0)
    before = jnp.where(iota((toks, toks), 0) < iota((toks, toks), 1), 1.0, 0.0).astype(BF16)
    ranks = dot(hits.astype(BF16), before)
    rank = jnp.sum(ranks * hits, axis=0, keepdims=True)
    target = owner * slots + rank
    picks = jnp.where(target == iota((n * slots, toks), 0).astype(F32), 1.0, 0.0).astype(BF16)
    which = iota((64, toks), 0)
    places = jnp.where(which == 0, place_row + 1.0, jnp.where(which == 1, column, 0.0)).astype(BF16)
    packed = jnp.concatenate(
        [dot(picks, lat_ref[...]), dot(picks, places, ((1,), (1,)))], axis=1
    ).astype(BF16)
    pack[...] = packed.reshape(n, slots, 128)
    arrived[pl.ds(me, 1)] = pack[pl.ds(me, 1)]
    pl.semaphore_wait(barrier, n - 1)
    copies = []
    for delta in range(1, n):
        to = lax.rem(me + delta, n)
        copy = pltpu.make_async_remote_copy(
            src_ref=pack.at[to], dst_ref=arrived.at[me],
            send_sem=send_a.at[delta - 1], recv_sem=recv_a.at[delta - 1],
            device_id={"sp": to}, device_id_type=pl.DeviceIdType.MESH,
        )
        copy.start()
        copies.append(copy)
    for copy in copies:
        copy.wait()
    got = arrived[...].reshape(n * slots, 128)
    got32 = got.astype(F32)
    ident = (got32[:, 64:65] - 1.0) * HALF_W + got32[:, 65:66]
    tokens = got[:, :64]
    odd = (iota((C_LAT, W), 1) & 1) == 1
    half = (iota((1, W), 1) >> 1).astype(F32)
    pieces = []
    for line_in in range(TB * HALF_ROWS):
        spots = jnp.where(ident == half + float(line_in * HALF_W), 1.0, 0.0).astype(BF16)
        grid = dot(tokens, spots, ((0,), (0,)))
        for a in range(2):
            base = a * 2 * C_LAT
            pieces.append(
                jnp.where(odd, grid[base + C_LAT: base + 2 * C_LAT], grid[base: base + C_LAT])
            )
    tile = jnp.concatenate(pieces, axis=0).T.astype(BF16)
    mine[...] = tile

    e = lax.rem(me + OFFSET_TILES, n)
    band_i = lax.rem(e, HBANDS)
    block_i = e // HBANDS
    blocks = n // HBANDS
    for phase in range(3):
        for k in range(depth):
            for side in range(3):
                if k == 0 and side == 1:
                    if phase == 0:
                        out_ref[1] = tile
                    continue
                slot = k * 3 + side
                shift = side - 1
                reader = lax.rem(me + k * HBANDS - shift + n, n)
                send_ok = (block_i + k < blocks)
                if shift == 1:
                    send_ok &= band_i > 0
                if shift == -1:
                    send_ok &= band_i < HBANDS - 1
                recv_ok = block_i >= k
                if shift == 1:
                    recv_ok &= band_i < HBANDS - 1
                if shift == -1:
                    recv_ok &= band_i > 0
                copy = pltpu.make_async_remote_copy(
                    src_ref=mine, dst_ref=near.at[slot],
                    send_sem=send_b.at[slot], recv_sem=recv_b.at[slot],
                    device_id={"sp": reader}, device_id_type=pl.DeviceIdType.MESH,
                )
                if phase == 0:
                    pl.when(send_ok)(copy.start)
                elif phase == 1:
                    def take():
                        copy.wait_recv()
                        out_ref[slot] = near[slot]

                    def blank():
                        out_ref[slot] = jnp.zeros_like(tile)

                    pl.when(recv_ok)(take)
                    pl.when(jnp.logical_not(recv_ok))(blank)
                else:
                    pl.when(send_ok)(copy.wait_send)


def gathered(latents, row_cell):
    n = lax.axis_size("sp")
    toks = latents.shape[0]
    slots = -(-2 * (toks // n) // 16) * 16
    depth = min(3, n // HBANDS)
    return pl.pallas_call(
        functools.partial(gather_kernel, n, slots, depth),
        out_shape=jax.ShapeDtypeStruct((depth * 3, W, 128), BF16),
        in_specs=[pl.BlockSpec(memory_space=pltpu.VMEM)] * 2,
        out_specs=pl.BlockSpec(memory_space=pltpu.VMEM),
        scratch_shapes=[
            pltpu.VMEM((n, slots, 128), BF16),
            pltpu.VMEM((n, slots, 128), BF16),
            pltpu.VMEM((W, 128), BF16),
            pltpu.VMEM((depth * 3, W, 128), BF16),
            pltpu.SemaphoreType.DMA((n - 1,)),
            pltpu.SemaphoreType.DMA((n - 1,)),
            pltpu.SemaphoreType.DMA((depth * 3,)),
            pltpu.SemaphoreType.DMA((depth * 3,)),
        ],
        compiler_params=pltpu.CompilerParams(collective_id=0, has_side_effects=True),
        name="gather_tiles",
    )(latents, row_cell.reshape(1, toks))


def shifted(x):
    where = iota(x.shape, 0)
    right = jnp.where(where == 0, 0.0, pltpu.roll(x, 1, 0))
    left = jnp.where(where == W - 1, 0.0, pltpu.roll(x, W - 1, 0))
    return right, left


def conv_kernel(n, depth, near_ref, w_in_ref, b_in_ref, gain_ref, b_mid_ref, w_mid_ref, out_ref,
                wide, acts, wcat, hidden_ref, acc, sems):
    mid = b_in_ref.shape[1]
    frames = TB + 2
    copies = []
    for index, (half, position, tap) in enumerate(((0, 1, 0), (0, 0, 1), (1, 1, 1), (1, 0, 2))):
        copy = pltpu.make_async_copy(
            w_mid_ref.at[tap], wcat.at[half, :, :, pl.ds(position * mid, mid)], sems.at[index]
        )
        copy.start()
        copies.append(copy)
    e = lax.rem(lax.axis_index("sp") + OFFSET_TILES, n)
    band_i = lax.rem(e, HBANDS)
    block_i = e // HBANDS
    lane = iota((W, 128), 1)
    source = iota((384, 1), 0)
    spread_to = ((source >> 4) & 7) * 48 + (source >> 7) * 16 + (source & 15)
    spread = jnp.where(spread_to == iota((384, 384), 1), 1.0, 0.0).astype(BF16)
    for k in range(3):
        for f in range(TB):
            t = (2 - k) * TB + f
            if k >= depth:
                wide[t] = jnp.zeros((W, 384), BF16)
                continue
            up, own, down = [near_ref[3 * k + side].astype(F32) for side in range(3)]
            x = jnp.where(
                lane < 32, pltpu.roll(up, 96 - 64 * f, 1),
                jnp.where(lane < 96, pltpu.roll(own, (32 - 64 * f) % 128, 1),
                          pltpu.roll(down, (96 - 64 * f) % 128, 1)),
            )
            right, left = shifted(x)
            rows = jnp.concatenate([right, x, left], axis=1).astype(BF16)
            wide[t] = dot(rows, spread).astype(BF16)

    kernel_in = w_in_ref[...]

    def first(t, carry):
        valid_t = block_i * TB - 2 + t >= 0
        for hh in range(HB + 2):
            lhs = jnp.concatenate(
                [wide[t + dt, :, hh * 48: hh * 48 + 144] for dt in range(3)], axis=1
            )
            hidden = (dot(lhs, kernel_in) + b_in_ref[...]).astype(BF16)
            hidden_ref[t, hh] = hidden
            v = hidden.astype(F32)
            scale = lax.rsqrt(jnp.mean(v * v, axis=-1, keepdims=True) + 1e-06)
            valid = valid_t
            if hh == 0:
                valid = valid_t & (band_i > 0)
            if hh == HB + 1:
                valid = valid_t & (band_i < HBANDS - 1)
            z = v * scale * gain_ref[...]
            act = jnp.where(valid, 0.5 * z * (1.0 + jnp.tanh(0.5 * z)), 0.0)
            right, left = shifted(act)
            acts[t, hh, :, :mid] = right.astype(BF16)
            acts[t, hh, :, mid: 2 * mid] = act.astype(BF16)
            acts[t, hh, :, 2 * mid:] = left.astype(BF16)
        return carry

    lax.fori_loop(0, frames, first, 0)
    for copy in copies:
        copy.wait()
    rows = HB * W
    for f in range(TB):
        acc[:, f * mid: (f + 1) * mid] = (
            hidden_ref[f + 2, 1: HB + 1].reshape(rows, mid).astype(F32) + b_mid_ref[...]
        )

    def second(dh, carry):
        def lhs(frame):
            return acts[frame, pl.ds(dh, HB)].reshape(rows, 3 * mid)

        acc[...] += dot(lhs(1), wcat[0, dh]) + dot(lhs(2), wcat[1, dh])
        acc[:, :mid] += dot(lhs(0), wcat[0, dh, :, mid:])
        acc[:, mid:] += dot(lhs(3), wcat[1, dh, :, :mid])
        return carry

    lax.fori_loop(0, 3, second, 0)
    for f in range(TB):
        out_ref[0, f] = acc[:, f * mid: (f + 1) * mid].astype(BF16).reshape(HB, W, mid)


def shards(latents, row_cell, w_in, b_in, gain, w_mid, b_mid):
    n = lax.axis_size("sp")
    near = gathered(latents, row_cell)
    mid = b_in.shape[0]
    vmem = pl.BlockSpec(memory_space=pltpu.VMEM)
    return pl.pallas_call(
        functools.partial(conv_kernel, n, near.shape[0] // 3),
        out_shape=jax.ShapeDtypeStruct((1, TB, HB, W, mid), BF16),
        in_specs=[vmem] * 5 + [pl.BlockSpec(memory_space=pl.ANY)],
        out_specs=vmem,
        scratch_shapes=[
            pltpu.VMEM((TB + 4, W, 384), BF16),
            pltpu.VMEM((TB + 2, HB + 2, W, 3 * mid), BF16),
            pltpu.VMEM((2, 3, 3 * mid, 2 * mid), BF16),
            pltpu.VMEM((TB + 2, HB + 2, W, mid), BF16),
            pltpu.VMEM((HB * W, TB * mid), F32),
            pltpu.SemaphoreType.DMA((4,)),
        ],
        compiler_params=pltpu.CompilerParams(vmem_limit_bytes=60 * 2**20),
        name="conv_block",
    )(
        near, w_in.reshape(27 * C_LAT, mid), b_in.reshape(1, mid), gain.reshape(1, mid),
        b_mid.reshape(1, mid), w_mid.reshape(3, 3, 3 * mid, mid),
    )


def solution(mesh):
    return jax.shard_map(
        shards,
        mesh=mesh,
        in_specs=(P(("grp", "sp"), None), P(("grp", "sp")), P(), P(), P(), P(), P()),
        out_specs=P(("grp", "sp"), None, None, None, None),
        check_vma=False,
    )
```

time: 125 us -> 47.8 us (0.38)
  matrix products: 64.6 us -> 0 us
  Pallas kernels: 0 us -> 40.8 us
  starting transfers between devices: 18.1 us -> 0 us
  waiting for transfers between devices: 13.8 us -> 0 us
  local copies, waits for them, and re-layouts: 20 us -> 6.55 us
  other arithmetic: 7.33 us -> 0 us
    dot_general x18 -> x0, matrix products: 64.6 us -> none  [causal_conv(): jnp.einsum('thwc,cd->thwd', window, kernel, preferred_element_type=jnp.fl...]
    pallas_call x0 -> x2, Pallas kernels: none -> 40.8 us  [the longest x1 21.7 us: shards(): pl.pallas_call(functools.partial(conv_kernel, n, near.shape[0] // 3), out...]
    all_to_all x2 -> x0, starting transfers between devices: 13.4 us -> none  [the longest x1 7.41 us: shards(): lax.all_to_all(places.reshape(devices, slot_count), 'sp', split_axis=0, c...]
    scatter x4 -> x0, local copies, waits for them, and re-layouts: 8.61 us -> none  [the longest x2 4.32 us: shards(): jnp.zeros((TOKS, channels_in), latents.dtype).at[flat_places]]
    slice x6 -> x0, local copies, waits for them, and re-layouts: 8.48 us -> none  [the longest x2 5.44 us: causal_conv(): kernel = weight[tap_time, tap_row].reshape(3 * channels, outputs)]
    ppermute x4 -> x0, waiting for transfers between devices: 7.91 us -> none  [the longest x2 5.62 us: passed_along(): return lax.ppermute(value, axis, pairs)]
    all_to_all x2 -> x0, waiting for transfers between devices: 5.88 us -> none  [the longest x1 5.88 us: shards(): lax.all_to_all(outgoing.reshape(devices, slot_count, channels_in), 'sp',...]
    ppermute x4 -> x0, starting transfers between devices: 4.7 us -> none  [the longest x1 4.43 us: with_halo(): lax.ppermute(lax.slice_in_dim(block, 0, width, axis=dim), axis, backward)]
  transfers between devices with their start and end apart: 6 -> 0, of which waited for: 3 -> 0; matrix products, arithmetic and copies ran while one was open for 7% -> 0% of each run, Pallas kernels for 0% -> 0%
where the time goes in v1:
time: 47.8 us; the launch traced here: 47.4 us
  Pallas kernels  40.8 us (85%)
  local copies, waits for them, and re-layouts  6.55 us (14%)
    pallas_call x1, Pallas kernels, shards(): pl.pallas_call(functools.partial(conv_kernel, n, near.shape[0] // 3), out...  21.7 us
    pallas_call x1, Pallas kernels, gathered(): pl.pallas_call(functools.partial(gather_kernel, n, slots, depth), out_sha...  19.1 us
    unnamed x1, local copies, waits for them, and re-layouts  1.54 us
    reshape x1, local copies, waits for them, and re-layouts, shards(): b_mid.reshape(1, mid)  1.28 us
    reshape x1, local copies, waits for them, and re-layouts, shards(): gain.reshape(1, mid)  1.26 us
    reshape x1, local copies, waits for them, and re-layouts, shards(): b_in.reshape(1, mid)  1.25 us
    reshape x1, local copies, waits for them, and re-layouts, gathered(): row_cell.reshape(1, toks)  1.23 us

profile of v1, /device:TPU:0, one launch (start us, length us, event | category | flops | bytes accessed | tf_op | source)
XLA Modules:
  0.0 47.4 jit_solution(12958854847962904761)
XLA Ops:
  0.0 1.2 %reshape.18.cell_ref = s32[1,320]{1,0:T(1,128)} reshape(s32[320]{0:T(512)} %param.8) | data formatting | bytes 2560 | tf_op jit(solution)/shard_map/reshape | solution.py:163
  1.2 1.3 %reshape.20.b_in_ref = f32[1,384]{1,0:T(1,128)} reshape(f32[384]{0:T(512)} %param.10) | data formatting | bytes 3072 | tf_op jit(solution)/shard_map/reshape | solution.py:276
  2.5 1.3 %reshape.21.gain_ref = f32[1,384]{1,0:T(1,128)} reshape(f32[384]{0:T(512)} %param.11) | data formatting | bytes 3072 | tf_op jit(solution)/shard_map/reshape | solution.py:276
  3.7 1.3 %reshape.22.b_mid_ref = f32[1,384]{1,0:T(1,128)} reshape(f32[384]{0:T(512)} %param.13) | data formatting | bytes 3072 | tf_op jit(solution)/shard_map/reshape | solution.py:277
  5.0 1.5 %copy.8.lat_ref = bf16[320,64]{1,0:T(8,128)(2,1)} copy(bf16[320,64]{0,1:T(8,128)(2,1)} %param.7) | data formatting | bytes 81920 | tf_op args[0]
  6.6 19.1 %gather_tiles.1.near_ref = bf16[6,160,128]{2,1,0:T(8,128)(2,1)} custom-call(bf16[320,64]{1,0:T(8,128)(2,1)} %copy.8.lat_ref, s32[1,320]{1,0:T(1,128)} %reshape.18.cell_ref), custom_call_target="tpu_custom_call" | custom-call | tf_op jit(solution)/shard_map/gather_tiles/pallas_call | solution.py:146
  25.7 21.7 %conv_block.1 = bf16[1,2,4,160,384]{4,3,2,1,0:T(8,128)(2,1)} custom-call(bf16[6,160,128]{2,1,0:T(8,128)(2,1)} %gather_tiles.1.near_ref, bf16[432,384]{1,0:T(8,128)(2,1)} %bitcast.3, f32[1,384]{1,0:T(1,128)} %reshape.20.b_in_ref, f32[1,384]{1,0:T(1,128)} %reshape.21.gain_ref, f32[1,384]{1,0:T(1,128)} %reshape.22.b_mid_ref, bf16[3,3,1152,384]{3,2,1,0:T(8,128)(2,1)} %bitcast.2), custom_call_target="tpu_custom_call" | custom-call | tf_op jit(solution)/shard_map/conv_block/pallas_call | solution.py:260

commit v2 on v1

--- a/solution.py
+++ b/solution.py
@@ -30,14 +30,14 @@
 def gather_kernel(n, slots, depth, lat_ref, cell_ref, out_ref, pack, arrived, mine, near,
                   send_a, recv_a, send_b, recv_b):
     me = lax.axis_index("sp")
-    toks = lat_ref.shape[0]
+    toks = lat_ref.shape[1]
     barrier = pltpu.get_barrier_semaphore()
     for delta in range(1, n):
         pl.semaphore_signal(
             barrier, inc=1, device_id={"sp": lax.rem(me + delta, n)},
             device_id_type=pl.DeviceIdType.MESH,
         )
-    cell = cell_ref[...].astype(F32)
+    cell = cell_ref[...].reshape(1, toks).astype(F32)
     line = jnp.floor((cell + 0.5) * (1.0 / HALF_W))
     column = cell - HALF_W * line
     token_rows = HALF_ROWS * HBANDS
@@ -57,9 +57,8 @@
     picks = jnp.where(target == iota((n * slots, toks), 0).astype(F32), 1.0, 0.0).astype(BF16)
     which = iota((64, toks), 0)
     places = jnp.where(which == 0, place_row + 1.0, jnp.where(which == 1, column, 0.0)).astype(BF16)
-    packed = jnp.concatenate(
-        [dot(picks, lat_ref[...]), dot(picks, places, ((1,), (1,)))], axis=1
-    ).astype(BF16)
+    packed = jnp.concatenate([lat_ref[...], places], axis=0)
+    packed = dot(picks, packed, ((1,), (1,))).astype(BF16)
     pack[...] = packed.reshape(n, slots, 128)
     arrived[pl.ds(me, 1)] = pack[pl.ds(me, 1)]
     pl.semaphore_wait(barrier, n - 1)
@@ -160,7 +159,7 @@
         ],
         compiler_params=pltpu.CompilerParams(collective_id=0, has_side_effects=True),
         name="gather_tiles",
-    )(latents, row_cell.reshape(1, toks))
+    )(latents.T, row_cell)
 
 
 def shifted(x):
@@ -172,7 +171,8 @@
 
 def conv_kernel(n, depth, near_ref, w_in_ref, b_in_ref, gain_ref, b_mid_ref, w_mid_ref, out_ref,
                 wide, acts, wcat, hidden_ref, acc, sems):
-    mid = b_in_ref.shape[1]
+    mid = b_in_ref.shape[0]
+    b_in, gain, b_mid = [ref[...].reshape(1, mid) for ref in (b_in_ref, gain_ref, b_mid_ref)]
     frames = TB + 2
     copies = []
     for index, (half, position, tap) in enumerate(((0, 1, 0), (0, 0, 1), (1, 1, 1), (1, 0, 2))):
@@ -212,7 +212,7 @@
             lhs = jnp.concatenate(
                 [wide[t + dt, :, hh * 48: hh * 48 + 144] for dt in range(3)], axis=1
             )
-            hidden = (dot(lhs, kernel_in) + b_in_ref[...]).astype(BF16)
+            hidden = (dot(lhs, kernel_in) + b_in).astype(BF16)
             hidden_ref[t, hh] = hidden
             v = hidden.astype(F32)
             scale = lax.rsqrt(jnp.mean(v * v, axis=-1, keepdims=True) + 1e-06)
@@ -221,7 +221,7 @@
                 valid = valid_t & (band_i > 0)
             if hh == HB + 1:
                 valid = valid_t & (band_i < HBANDS - 1)
-            z = v * scale * gain_ref[...]
+            z = v * scale * gain
             act = jnp.where(valid, 0.5 * z * (1.0 + jnp.tanh(0.5 * z)), 0.0)
             right, left = shifted(act)
             acts[t, hh, :, :mid] = right.astype(BF16)
@@ -235,7 +235,7 @@
     rows = HB * W
     for f in range(TB):
         acc[:, f * mid: (f + 1) * mid] = (
-            hidden_ref[f + 2, 1: HB + 1].reshape(rows, mid).astype(F32) + b_mid_ref[...]
+            hidden_ref[f + 2, 1: HB + 1].reshape(rows, mid).astype(F32) + b_mid
         )
 
     def second(dh, carry):
@@ -273,8 +273,7 @@
         compiler_params=pltpu.CompilerParams(vmem_limit_bytes=60 * 2**20),
         name="conv_block",
     )(
-        near, w_in.reshape(27 * C_LAT, mid), b_in.reshape(1, mid), gain.reshape(1, mid),
-        b_mid.reshape(1, mid), w_mid.reshape(3, 3, 3 * mid, mid),
+        near, w_in.reshape(27 * C_LAT, mid), b_in, gain, b_mid, w_mid.reshape(3, 3, 3 * mid, mid),
     )
 
 

time: 47.8 us -> 41.1 us (0.86)
  local copies, waits for them, and re-layouts: 6.55 us -> 0 us
    reshape x4 -> x0, local copies, waits for them, and re-layouts: 5.02 us -> none  [the longest x1 1.28 us: shards(): b_mid.reshape(1, mid)]
    unnamed x1 -> x0, local copies, waits for them, and re-layouts: 1.54 us -> none
where the time goes in v2:
time: 41.1 us; the launch traced here: 40.8 us
  Pallas kernels  40.8 us (99%)
    pallas_call x1, Pallas kernels, shards(): pl.pallas_call(functools.partial(conv_kernel, n, near.shape[0] // 3), out...  21.8 us
    pallas_call x1, Pallas kernels, gathered(): pl.pallas_call(functools.partial(gather_kernel, n, slots, depth), out_sha...  19 us

profile of v2, /device:TPU:0, one launch (start us, length us, event | category | flops | bytes accessed | tf_op | source)
XLA Modules:
  0.0 40.8 jit_solution(13580959974242683595)
XLA Ops:
  0.0 19.0 %gather_tiles.1.near_ref = bf16[6,160,128]{2,1,0:T(8,128)(2,1)} custom-call(bf16[64,320]{1,0:T(8,128)(2,1)} %bitcast.5, s32[320]{0:T(512)} %cell_ref.1), custom_call_target="tpu_custom_call" | custom-call | tf_op jit(solution)/shard_map/gather_tiles/pallas_call | solution.py:145
  19.0 21.8 %conv_block.1 = bf16[1,2,4,160,384]{4,3,2,1,0:T(8,128)(2,1)} custom-call(bf16[6,160,128]{2,1,0:T(8,128)(2,1)} %gather_tiles.1.near_ref, bf16[432,384]{1,0:T(8,128)(2,1)} %bitcast.4, f32[384]{0:T(512)} %b_in_ref.1, f32[384]{0:T(512)} %gain_ref.1, f32[384]{0:T(512)} %b_mid_ref.1, bf16[3,3,1152,384]{3,2,1,0:T(8,128)(2,1)} %bitcast.3), custom_call_target="tpu_custom_call" | custom-call | tf_op jit(solution)/shard_map/conv_block/pallas_call | solution.py:260

commit v3 on v2

--- a/solution.py
+++ b/solution.py
@@ -170,7 +170,7 @@
 
 
 def conv_kernel(n, depth, near_ref, w_in_ref, b_in_ref, gain_ref, b_mid_ref, w_mid_ref, out_ref,
-                wide, acts, wcat, hidden_ref, acc, sems):
+                wide, taps_in, scales, acts, wcat, hidden_ref, sems):
     mid = b_in_ref.shape[0]
     b_in, gain, b_mid = [ref[...].reshape(1, mid) for ref in (b_in_ref, gain_ref, b_mid_ref)]
     frames = TB + 2
@@ -186,13 +186,13 @@
     block_i = e // HBANDS
     lane = iota((W, 128), 1)
     source = iota((384, 1), 0)
-    spread_to = ((source >> 4) & 7) * 48 + (source >> 7) * 16 + (source & 15)
-    spread = jnp.where(spread_to == iota((384, 384), 1), 1.0, 0.0).astype(BF16)
+    spread_to = ((source >> 4) & 7) * 64 + (source >> 7) * 16 + (source & 15)
+    spread = jnp.where(spread_to == iota((384, 512), 1), 1.0, 0.0).astype(BF16)
     for k in range(3):
         for f in range(TB):
             t = (2 - k) * TB + f
             if k >= depth:
-                wide[t] = jnp.zeros((W, 384), BF16)
+                wide[t] = jnp.zeros((2, W, 512), BF16)
                 continue
             up, own, down = [near_ref[3 * k + side].astype(F32) for side in range(3)]
             x = jnp.where(
@@ -202,54 +202,82 @@
             )
             right, left = shifted(x)
             rows = jnp.concatenate([right, x, left], axis=1).astype(BF16)
-            wide[t] = dot(rows, spread).astype(BF16)
-
-    kernel_in = w_in_ref[...]
-
-    def first(t, carry):
+            lines = dot(rows, spread)
+            wide[t, 0] = lines.astype(BF16)
+            wide[t, 1] = pltpu.roll(lines, 448, 1).astype(BF16)
+
+    taps_in[...] = jnp.zeros_like(taps_in)
+    for dt in range(3):
+        for dh in range(3):
+            base = (dt * 3 + dh) * 48
+            taps_in[dt, dh * 64: dh * 64 + 48] = w_in_ref[base: base + 48]
+
+    half_gain = 0.5 * gain
+    pairs = (HB + 2) // 2
+    steps = frames * pairs
+
+    def convolve(step):
+        t = step // pairs
+        pair = lax.rem(step, pairs)
+        lanes = pl.ds(pl.multiple_of(pair * 128, 128), 256)
+        lhs = jnp.concatenate(
+            [wide[t + dt, :, :, lanes].reshape(2 * W, 256) for dt in range(3)], axis=1
+        )
+        hidden = (dot(lhs, taps_in[...].reshape(768, mid)) + b_in).astype(BF16)
+        hidden_ref[t, pl.ds(2 * pair, 2)] = hidden.reshape(2, W, mid)
+        v = hidden.astype(F32)
+        scale = lax.rsqrt(jnp.mean(v * v, axis=-1, keepdims=True) + 1e-06)
+        scales[...] = jnp.broadcast_to(scale, scales.shape)
+
+    def activate(step):
+        t = step // pairs
+        pair = lax.rem(step, pairs)
         valid_t = block_i * TB - 2 + t >= 0
-        for hh in range(HB + 2):
-            lhs = jnp.concatenate(
-                [wide[t + dt, :, hh * 48: hh * 48 + 144] for dt in range(3)], axis=1
-            )
-            hidden = (dot(lhs, kernel_in) + b_in).astype(BF16)
-            hidden_ref[t, hh] = hidden
-            v = hidden.astype(F32)
-            scale = lax.rsqrt(jnp.mean(v * v, axis=-1, keepdims=True) + 1e-06)
-            valid = valid_t
-            if hh == 0:
-                valid = valid_t & (band_i > 0)
-            if hh == HB + 1:
-                valid = valid_t & (band_i < HBANDS - 1)
-            z = v * scale * gain
-            act = jnp.where(valid, 0.5 * z * (1.0 + jnp.tanh(0.5 * z)), 0.0)
-            right, left = shifted(act)
+        for side in range(2):
+            hh = 2 * pair + side
+            v = hidden_ref[t, hh].astype(F32)
+            if side == 0:
+                valid = valid_t & ((band_i > 0) | (pair > 0))
+            else:
+                valid = valid_t & ((band_i < HBANDS - 1) | (pair < pairs - 1))
+            scale = jnp.where(valid, scales[side * W: (side + 1) * W, :1], 0.0)
+            z = v * scale * half_gain
+            act = z + z * jnp.tanh(z)
+            zero = jnp.zeros((1, mid), F32)
+            right = jnp.concatenate([zero, act[:-1]], axis=0)
+            left = jnp.concatenate([act[1:], zero], axis=0)
             acts[t, hh, :, :mid] = right.astype(BF16)
             acts[t, hh, :, mid: 2 * mid] = act.astype(BF16)
             acts[t, hh, :, 2 * mid:] = left.astype(BF16)
+
+    convolve(0)
+
+    def first(step, carry):
+        activate(step - 1)
+        convolve(step)
         return carry
 
-    lax.fori_loop(0, frames, first, 0)
+    lax.fori_loop(1, steps, first, 0)
+    activate(steps - 1)
     for copy in copies:
         copy.wait()
     rows = HB * W
+
+    def lhs(frame):
+        return jnp.concatenate(
+            [acts[frame, dh: dh + HB].reshape(rows, 3 * mid) for dh in range(3)], axis=1
+        )
+
+    def tap(half, lanes):
+        return wcat[half, :, :, lanes].reshape(9 * mid, -1)
+
+    both = slice(0, 2 * mid)
+    mixed = dot(lhs(1), tap(0, both)) + dot(lhs(2), tap(1, both))
+    edges = (dot(lhs(0), tap(0, slice(mid, 2 * mid))), dot(lhs(3), tap(1, slice(0, mid))))
     for f in range(TB):
-        acc[:, f * mid: (f + 1) * mid] = (
-            hidden_ref[f + 2, 1: HB + 1].reshape(rows, mid).astype(F32) + b_mid
-        )
-
-    def second(dh, carry):
-        def lhs(frame):
-            return acts[frame, pl.ds(dh, HB)].reshape(rows, 3 * mid)
-
-        acc[...] += dot(lhs(1), wcat[0, dh]) + dot(lhs(2), wcat[1, dh])
-        acc[:, :mid] += dot(lhs(0), wcat[0, dh, :, mid:])
-        acc[:, mid:] += dot(lhs(3), wcat[1, dh, :, :mid])
-        return carry
-
-    lax.fori_loop(0, 3, second, 0)
-    for f in range(TB):
-        out_ref[0, f] = acc[:, f * mid: (f + 1) * mid].astype(BF16).reshape(HB, W, mid)
+        total = mixed[:, f * mid: (f + 1) * mid] + edges[f] + b_mid
+        total += hidden_ref[f + 2, 1: HB + 1].reshape(rows, mid).astype(F32)
+        out_ref[0, f] = total.astype(BF16).reshape(HB, W, mid)
 
 
 def shards(latents, row_cell, w_in, b_in, gain, w_mid, b_mid):
@@ -263,11 +291,12 @@
         in_specs=[vmem] * 5 + [pl.BlockSpec(memory_space=pl.ANY)],
         out_specs=vmem,
         scratch_shapes=[
-            pltpu.VMEM((TB + 4, W, 384), BF16),
+            pltpu.VMEM((TB + 4, 2, W, 512), BF16),
+            pltpu.VMEM((3, 256, mid), BF16),
+            pltpu.VMEM((2 * W, 128), F32),
             pltpu.VMEM((TB + 2, HB + 2, W, 3 * mid), BF16),
             pltpu.VMEM((2, 3, 3 * mid, 2 * mid), BF16),
             pltpu.VMEM((TB + 2, HB + 2, W, mid), BF16),
-            pltpu.VMEM((HB * W, TB * mid), F32),
             pltpu.SemaphoreType.DMA((4,)),
         ],
         compiler_params=pltpu.CompilerParams(vmem_limit_bytes=60 * 2**20),

time: 41.1 us -> 41.8 us (1.017)
  Pallas kernels: 40.8 us -> 41.5 us
    pallas_call x1, Pallas kernels: 21.8 us -> 22.5 us  [shards(): pl.pallas_call(functools.partial(conv_kernel, n, near.shape[0] // 3), out...]
where the time goes in v3:
time: 41.8 us; the launch traced here: 41.5 us
  Pallas kernels  41.5 us (99%)
    pallas_call x1, Pallas kernels, shards(): pl.pallas_call(functools.partial(conv_kernel, n, near.shape[0] // 3), out...  22.5 us
    pallas_call x1, Pallas kernels, gathered(): pl.pallas_call(functools.partial(gather_kernel, n, slots, depth), out_sha...  19 us

profile of v3, /device:TPU:0, one launch (start us, length us, event | category | flops | bytes accessed | tf_op | source)
XLA Modules:
  0.0 41.5 jit_solution(16131487351376185618)
XLA Ops:
  0.0 19.0 %gather_tiles.1.near_ref = bf16[6,160,128]{2,1,0:T(8,128)(2,1)} custom-call(bf16[64,320]{1,0:T(8,128)(2,1)} %bitcast.5, s32[320]{0:T(512)} %cell_ref.1), custom_call_target="tpu_custom_call" | custom-call | tf_op jit(solution)/shard_map/gather_tiles/pallas_call | solution.py:145
  19.0 22.5 %conv_block.1 = bf16[1,2,4,160,384]{4,3,2,1,0:T(8,128)(2,1)} custom-call(bf16[6,160,128]{2,1,0:T(8,128)(2,1)} %gather_tiles.1.near_ref, bf16[432,384]{1,0:T(8,128)(2,1)} %bitcast.4, f32[384]{0:T(512)} %b_in_ref.1, f32[384]{0:T(512)} %gain_ref.1, f32[384]{0:T(512)} %b_mid_ref.1, bf16[3,3,1152,384]{3,2,1,0:T(8,128)(2,1)} %bitcast.3), custom_call_target="tpu_custom_call" | custom-call | tf_op jit(solution)/shard_map/conv_block/pallas_call | solution.py:288

commit v4 on v2

--- a/solution.py
+++ b/solution.py
@@ -27,7 +27,8 @@
     return lax.dot_general(a, b, (dims, ((), ())), preferred_element_type=F32)
 
 
-def gather_kernel(n, slots, depth, lat_ref, cell_ref, out_ref, pack, arrived, mine, near,
+def gather_kernel(n, per, height, depth, lat_ref, cell_ref, out_ref, pack, arrived, mine, above,
+                  below, near,
                   send_a, recv_a, send_b, recv_b):
     me = lax.axis_index("sp")
     toks = lat_ref.shape[1]
@@ -53,13 +54,26 @@
     before = jnp.where(iota((toks, toks), 0) < iota((toks, toks), 1), 1.0, 0.0).astype(BF16)
     ranks = dot(hits.astype(BF16), before)
     rank = jnp.sum(ranks * hits, axis=0, keepdims=True)
-    target = owner * slots + rank
-    picks = jnp.where(target == iota((n * slots, toks), 0).astype(F32), 1.0, 0.0).astype(BF16)
-    which = iota((64, toks), 0)
-    places = jnp.where(which == 0, place_row + 1.0, jnp.where(which == 1, column, 0.0)).astype(BF16)
-    packed = jnp.concatenate([lat_ref[...], places], axis=0)
-    packed = dot(picks, packed, ((1,), (1,))).astype(BF16)
-    pack[...] = packed.reshape(n, slots, 128)
+    dest = iota((n, height, toks), 0).astype(F32)
+    row = iota((n, height, toks), 1).astype(F32)
+    hit = owner.reshape(1, 1, toks) == dest
+    rank3 = rank.reshape(1, 1, toks)
+
+    def block(value):
+        return value.reshape(n * height, toks).astype(BF16)
+
+    low = block(jnp.where(hit & (rank3 == row) & (row < per), 1.0, 0.0))
+    high = block(jnp.where(hit & (rank3 == row + per) & (row < per), 1.0, 0.0))
+    notes = jnp.where(row == per, place_row.reshape(1, 1, toks) + 1.0,
+                      jnp.where(row == per + 1, column.reshape(1, 1, toks), 0.0))
+    notes = block(jnp.where(hit, notes, 0.0))
+    lane_of = jnp.where(rank < per, rank, rank + float(height - per))
+    lanes = jnp.where(lane_of == iota((128, toks), 0).astype(F32), 1.0, 0.0).astype(BF16)
+    nt = ((1,), (1,))
+    packed = jnp.concatenate(
+        [dot(low, lat_ref[...], nt), dot(high, lat_ref[...], nt)], axis=1
+    ) + dot(notes, lanes, nt)
+    pack[...] = packed.reshape(n, height, 128).astype(BF16)
     arrived[pl.ds(me, 1)] = pack[pl.ds(me, 1)]
     pl.semaphore_wait(barrier, n - 1)
     copies = []
@@ -74,16 +88,25 @@
         copies.append(copy)
     for copy in copies:
         copy.wait()
-    got = arrived[...].reshape(n * slots, 128)
-    got32 = got.astype(F32)
-    ident = (got32[:, 64:65] - 1.0) * HALF_W + got32[:, 65:66]
-    tokens = got[:, :64]
+    got3 = arrived[...].astype(F32)
+    got = got3.reshape(n * height, 128).astype(BF16)
+    unit = jnp.where(iota((2 * height, 128), 0) == iota((2 * height, 128), 1), 1.0, 0.0).astype(BF16)
+    ident = (
+        (dot(unit, got3[:, per].astype(BF16), nt) - 1.0) * HALF_W
+        + dot(unit, got3[:, per + 1].astype(BF16), nt)
+    )
+    idents = [
+        jnp.concatenate([ident[h * height: (h + 1) * height, s: s + 1] for s in range(n)], axis=0)
+        for h in range(2)
+    ]
     odd = (iota((C_LAT, W), 1) & 1) == 1
     half = (iota((1, W), 1) >> 1).astype(F32)
     pieces = []
     for line_in in range(TB * HALF_ROWS):
-        spots = jnp.where(ident == half + float(line_in * HALF_W), 1.0, 0.0).astype(BF16)
-        grid = dot(tokens, spots, ((0,), (0,)))
+        grid = 0.0
+        for h in range(2):
+            spots = jnp.where(idents[h] == half + float(line_in * HALF_W), 1.0, 0.0).astype(BF16)
+            grid += dot(got[:, 64 * h: 64 * h + 64], spots, ((0,), (0,)))
         for a in range(2):
             base = a * 2 * C_LAT
             pieces.append(
@@ -91,6 +114,9 @@
             )
     tile = jnp.concatenate(pieces, axis=0).T.astype(BF16)
     mine[...] = tile
+    for edge, top in ((above, HB - 2), (below, 0)):
+        rim = jnp.concatenate([pieces[f * HB + top + r] for f in range(TB) for r in range(2)], axis=0)
+        edge[...] = jnp.concatenate([rim[:, :HALF_W], rim[:, HALF_W:]], axis=0).T.astype(BF16)
 
     e = lax.rem(me + OFFSET_TILES, n)
     band_i = lax.rem(e, HBANDS)
@@ -101,9 +127,11 @@
             for side in range(3):
                 if k == 0 and side == 1:
                     if phase == 0:
-                        out_ref[1] = tile
+                        out_ref[0, :W] = tile
                     continue
                 slot = k * 3 + side
+                start, size = ((W, HALF_W), (0, W), (W + HALF_W, HALF_W))[side]
+                part = pl.ds(start, size)
                 shift = side - 1
                 reader = lax.rem(me + k * HBANDS - shift + n, n)
                 send_ok = (block_i + k < blocks)
@@ -117,7 +145,7 @@
                 if shift == -1:
                     recv_ok &= band_i > 0
                 copy = pltpu.make_async_remote_copy(
-                    src_ref=mine, dst_ref=near.at[slot],
+                    src_ref=(above, mine, below)[side], dst_ref=near.at[k, part],
                     send_sem=send_b.at[slot], recv_sem=recv_b.at[slot],
                     device_id={"sp": reader}, device_id_type=pl.DeviceIdType.MESH,
                 )
@@ -126,10 +154,10 @@
                 elif phase == 1:
                     def take():
                         copy.wait_recv()
-                        out_ref[slot] = near[slot]
+                        out_ref[k, part] = near[k, part]
 
                     def blank():
-                        out_ref[slot] = jnp.zeros_like(tile)
+                        out_ref[k, part] = jnp.zeros((size, 128), BF16)
 
                     pl.when(recv_ok)(take)
                     pl.when(jnp.logical_not(recv_ok))(blank)
@@ -140,18 +168,21 @@
 def gathered(latents, row_cell):
     n = lax.axis_size("sp")
     toks = latents.shape[0]
-    slots = -(-2 * (toks // n) // 16) * 16
+    per = toks // n
+    height = -(-(per + 2) // 8) * 8
     depth = min(3, n // HBANDS)
     return pl.pallas_call(
-        functools.partial(gather_kernel, n, slots, depth),
-        out_shape=jax.ShapeDtypeStruct((depth * 3, W, 128), BF16),
+        functools.partial(gather_kernel, n, per, height, depth),
+        out_shape=jax.ShapeDtypeStruct((depth, 2 * W, 128), BF16),
         in_specs=[pl.BlockSpec(memory_space=pltpu.VMEM)] * 2,
         out_specs=pl.BlockSpec(memory_space=pltpu.VMEM),
         scratch_shapes=[
-            pltpu.VMEM((n, slots, 128), BF16),
-            pltpu.VMEM((n, slots, 128), BF16),
+            pltpu.VMEM((n, height, 128), BF16),
+            pltpu.VMEM((n, height, 128), BF16),
             pltpu.VMEM((W, 128), BF16),
-            pltpu.VMEM((depth * 3, W, 128), BF16),
+            pltpu.VMEM((HALF_W, 128), BF16),
+            pltpu.VMEM((HALF_W, 128), BF16),
+            pltpu.VMEM((depth, 2 * W, 128), BF16),
             pltpu.SemaphoreType.DMA((n - 1,)),
             pltpu.SemaphoreType.DMA((n - 1,)),
             pltpu.SemaphoreType.DMA((depth * 3,)),
@@ -170,7 +201,7 @@
 
 
 def conv_kernel(n, depth, near_ref, w_in_ref, b_in_ref, gain_ref, b_mid_ref, w_mid_ref, out_ref,
-                wide, acts, wcat, hidden_ref, acc, sems):
+                wide, acts, wcat, hidden_ref, sems):
     mid = b_in_ref.shape[0]
     b_in, gain, b_mid = [ref[...].reshape(1, mid) for ref in (b_in_ref, gain_ref, b_mid_ref)]
     frames = TB + 2
@@ -194,11 +225,16 @@
             if k >= depth:
                 wide[t] = jnp.zeros((W, 384), BF16)
                 continue
-            up, own, down = [near_ref[3 * k + side].astype(F32) for side in range(3)]
+            own = near_ref[k, :W].astype(F32)
+            up, down = [
+                jnp.concatenate([pltpu.roll(rim, (to - 32 * f) % 128, 1),
+                                 pltpu.roll(rim, (to - 64 - 32 * f) % 128, 1)], axis=0)
+                for rim, to in ((near_ref[k, W: W + HALF_W].astype(F32), 0),
+                                (near_ref[k, W + HALF_W:].astype(F32), 96))
+            ]
             x = jnp.where(
-                lane < 32, pltpu.roll(up, 96 - 64 * f, 1),
-                jnp.where(lane < 96, pltpu.roll(own, (32 - 64 * f) % 128, 1),
-                          pltpu.roll(down, (96 - 64 * f) % 128, 1)),
+                lane < 32, up,
+                jnp.where(lane < 96, pltpu.roll(own, (32 - 64 * f) % 128, 1), down),
             )
             right, left = shifted(x)
             rows = jnp.concatenate([right, x, left], axis=1).astype(BF16)
@@ -233,23 +269,22 @@
     for copy in copies:
         copy.wait()
     rows = HB * W
+
+    def lhs(frame):
+        return jnp.concatenate(
+            [acts[frame, dh: dh + HB].reshape(rows, 3 * mid) for dh in range(3)], axis=1
+        )
+
+    def tap(half, lanes):
+        return wcat[half, :, :, lanes].reshape(9 * mid, -1)
+
+    both = slice(0, 2 * mid)
+    mixed = dot(lhs(1), tap(0, both)) + dot(lhs(2), tap(1, both))
+    edges = (dot(lhs(0), tap(0, slice(mid, 2 * mid))), dot(lhs(3), tap(1, slice(0, mid))))
     for f in range(TB):
-        acc[:, f * mid: (f + 1) * mid] = (
-            hidden_ref[f + 2, 1: HB + 1].reshape(rows, mid).astype(F32) + b_mid
-        )
-
-    def second(dh, carry):
-        def lhs(frame):
-            return acts[frame, pl.ds(dh, HB)].reshape(rows, 3 * mid)
-
-        acc[...] += dot(lhs(1), wcat[0, dh]) + dot(lhs(2), wcat[1, dh])
-        acc[:, :mid] += dot(lhs(0), wcat[0, dh, :, mid:])
-        acc[:, mid:] += dot(lhs(3), wcat[1, dh, :, :mid])
-        return carry
-
-    lax.fori_loop(0, 3, second, 0)
-    for f in range(TB):
-        out_ref[0, f] = acc[:, f * mid: (f + 1) * mid].astype(BF16).reshape(HB, W, mid)
+        total = mixed[:, f * mid: (f + 1) * mid] + edges[f] + b_mid
+        total += hidden_ref[f + 2, 1: HB + 1].reshape(rows, mid).astype(F32)
+        out_ref[0, f] = total.astype(BF16).reshape(HB, W, mid)
 
 
 def shards(latents, row_cell, w_in, b_in, gain, w_mid, b_mid):
@@ -258,7 +293,7 @@
     mid = b_in.shape[0]
     vmem = pl.BlockSpec(memory_space=pltpu.VMEM)
     return pl.pallas_call(
-        functools.partial(conv_kernel, n, near.shape[0] // 3),
+        functools.partial(conv_kernel, n, near.shape[0]),
         out_shape=jax.ShapeDtypeStruct((1, TB, HB, W, mid), BF16),
         in_specs=[vmem] * 5 + [pl.BlockSpec(memory_space=pl.ANY)],
         out_specs=vmem,
@@ -267,7 +302,6 @@
             pltpu.VMEM((TB + 2, HB + 2, W, 3 * mid), BF16),
             pltpu.VMEM((2, 3, 3 * mid, 2 * mid), BF16),
             pltpu.VMEM((TB + 2, HB + 2, W, mid), BF16),
-            pltpu.VMEM((HB * W, TB * mid), F32),
             pltpu.SemaphoreType.DMA((4,)),
         ],
         compiler_params=pltpu.CompilerParams(vmem_limit_bytes=60 * 2**20),

time: 41.1 us -> 37.9 us (0.922)
  Pallas kernels: 40.8 us -> 37.7 us
    pallas_call x2, Pallas kernels: 40.8 us -> 37.7 us  [the longest x1 20.4 us: shards(): pl.pallas_call(functools.partial(conv_kernel, n, near.shape[0]), out_shap...]
where the time goes in v4:
time: 37.9 us; the launch traced here: 37.7 us
  Pallas kernels  37.7 us (99%)
    pallas_call x1, Pallas kernels, shards(): pl.pallas_call(functools.partial(conv_kernel, n, near.shape[0]), out_shap...  20.4 us
    pallas_call x1, Pallas kernels, gathered(): pl.pallas_call(functools.partial(gather_kernel, n, per, height, depth), o...  17.3 us

profile of v4, /device:TPU:0, one launch (start us, length us, event | category | flops | bytes accessed | tf_op | source)
XLA Modules:
  0.0 37.7 jit_solution(13126822400201255565)
XLA Ops:
  0.0 17.3 %gather_tiles.1.near_ref = bf16[2,320,128]{2,1,0:T(8,128)(2,1)} custom-call(bf16[64,320]{1,0:T(8,128)(2,1)} %bitcast.5, s32[320]{0:T(512)} %cell_ref.1), custom_call_target="tpu_custom_call" | custom-call | tf_op jit(solution)/shard_map/gather_tiles/pallas_call | solution.py:174
  17.3 20.4 %conv_block.1 = bf16[1,2,4,160,384]{4,3,2,1,0:T(8,128)(2,1)} custom-call(bf16[2,320,128]{2,1,0:T(8,128)(2,1)} %gather_tiles.1.near_ref, bf16[432,384]{1,0:T(8,128)(2,1)} %bitcast.4, f32[384]{0:T(512)} %b_in_ref.1, f32[384]{0:T(512)} %gain_ref.1, f32[384]{0:T(512)} %b_mid_ref.1, bf16[3,3,1152,384]{3,2,1,0:T(8,128)(2,1)} %bitcast.3), custom_call_target="tpu_custom_call" | custom-call | tf_op jit(solution)/shard_map/conv_block/pallas_call | solution.py:295
